TPU v7x, 32 devices: a whole 2x2x4 slice. The times are simulated.
32 devices in a mesh: groups: 2 (over y), ctx: 4 (over z), enc: 2 (over x), tp: 2 (over core).
Axes of the slice: x: 2, y: 2, z: 4, core: 2. Of those that a mesh axis runs over, the one named last changes fastest.
Arguments:
- enc_rows: bfloat16 [4, 1024, 1280], P(('groups', 'enc'), 'ctx'), parts along dimension 0, may hold values from -6 to 6
- row_slot: int32 [4, 1024], P(('groups', 'enc'), 'ctx'), parts along dimension 0, may hold values from 0 to 1023, as said below
- row_kind: int32 [4, 1024], P(('groups', 'enc'), 'ctx'), parts along dimension 0, may hold values from 0 to 1, as said below
- audio_proj: bfloat16 [1280, 8192], P(None, ('ctx', 'tp')), may hold values from -0.15625 to 0.15625
- frame_proj: bfloat16 [1280, 8192], P(None, ('ctx', 'tp')), may hold values from -0.15625 to 0.15625
- audio_bias: bfloat16 [8192], P(('ctx', 'tp')), may hold values from -3 to 3
- frame_bias: bfloat16 [8192], P(('ctx', 'tp')), may hold values from -3 to 3
- norm_gain: bfloat16 [8192], replicated, may hold values from 0.5 to 1.5
Outputs:
- normed: bfloat16 [4, 1024, 8192], P(('groups', 'enc'), ('ctx', 'tp')), parts along dimension 0
There are 2 independent parts, one for each index of `groups`. A program takes and returns all parts, laid end to end along the dimension named above; an argument that names none is the same for every part. Nothing has to cross between parts.
Inputs may be any that keep to these rules, and one draw needn't show every extreme that they name: `row_slot`: in each conversation every value appears exactly once. A row with value s fills context shard s // 256. Of the 256 rows of one owner (one index of ctx, in one conversation), at most 128 fill any one context shard, and every owner sends exactly 128 rows to some context shard. Rows come in 2-second spans of at most 128 rows: one span's rows are consecutive at the owner and fill consecutive positions. `row_kind`: within a span the audio rows come before the frame rows.
All inputs are finite; a program needn't handle non-finite values.
Results may differ from a plain program's by a relative error of at most 0.005.
Values may be sent and summed in bfloat16 or wider, within the bound.
No kernel may reach another device: no remote copies, remote signals or barrier semaphores. Data moves between devices by JAX's collectives and lax.ppermute only.
A program may use at most 128 MiB of HBM per device.

v0:
```python
import jax
import jax.numpy as jnp
from jax import lax
from jax.sharding import PartitionSpec as P


def project(enc_part, kind_part, weights, bias_audio, bias_frame):
    is_audio = (kind_part == 0)[:, None]
    nothing = jnp.zeros((), enc_part.dtype)
    stacked = jnp.concatenate(
        [jnp.where(is_audio, enc_part, nothing), jnp.where(is_audio, nothing, enc_part)], axis=1
    )
    result = jnp.dot(stacked, weights, preferred_element_type=jnp.float32)
    return result + jnp.where(is_audio, bias_audio[None, :], bias_frame[None, :])


def body(enc_rows, row_slot, row_kind, audio_proj, frame_proj, audio_bias, frame_bias, norm_gain):
    owned_rows = enc_rows[0]
    owned_slot = row_slot[0]
    owned_kind = row_kind[0]
    seq_dev = owned_rows.shape[0]
    width_enc = owned_rows.shape[1]
    n_ctx = lax.axis_size("ctx")
    capacity = 2 * seq_dev // n_ctx
    target = owned_slot // seq_dev
    position = owned_slot % seq_dev
    onehot = (target[:, None] == jnp.arange(n_ctx, dtype=jnp.int32)[None, :]).astype(jnp.int32)
    before = jnp.cumsum(onehot, axis=0) - onehot
    ranking = jnp.sum(before * onehot, axis=1)
    send_index = target * capacity + ranking
    outgoing = n_ctx * capacity
    select_send = send_index[None, :] == jnp.arange(outgoing, dtype=jnp.int32)[:, None]
    parcel = jnp.dot(
        select_send.astype(jnp.bfloat16), owned_rows, preferred_element_type=jnp.float32
    )
    parcel = parcel.astype(jnp.bfloat16).reshape(n_ctx, capacity, width_enc)
    send_int = select_send.astype(jnp.int32)
    where_to = (jnp.sum(send_int * (position + 1)[None, :], axis=1) - 1).reshape(n_ctx, capacity)
    what_kind = jnp.sum(send_int * owned_kind[None, :], axis=1).reshape(n_ctx, capacity)
    arrived = (
        lax.all_to_all(parcel, "ctx", split_axis=0, concat_axis=0, tiled=True),
        lax.all_to_all(where_to, "ctx", split_axis=0, concat_axis=0, tiled=True),
        lax.all_to_all(what_kind, "ctx", split_axis=0, concat_axis=0, tiled=True),
    )
    rows_in = arrived[0].reshape(outgoing, width_enc)
    pos_in = arrived[1].reshape(outgoing)
    kind_in = arrived[2].reshape(outgoing)
    select_land = pos_in[None, :] == jnp.arange(seq_dev, dtype=jnp.int32)[:, None]
    shard_rows = jnp.dot(
        select_land.astype(jnp.bfloat16), rows_in, preferred_element_type=jnp.float32
    ).astype(jnp.bfloat16)
    shard_kind = jnp.sum(select_land.astype(jnp.int32) * kind_in[None, :], axis=1)
    weights = jnp.concatenate([audio_proj, frame_proj], axis=0)
    bias_audio = audio_bias.astype(jnp.float32)
    bias_frame = frame_bias.astype(jnp.float32)
    columns = project(
        lax.all_gather(shard_rows, "ctx", axis=0, tiled=True),
        lax.all_gather(shard_kind, "ctx", axis=0, tiled=True),
        weights,
        bias_audio,
        bias_frame,
    )
    embeds = lax.all_to_all(
        columns.astype(jnp.bfloat16), ("ctx", "tp"), split_axis=0, concat_axis=1, tiled=True
    )
    widened = embeds.astype(jnp.float32)
    mean_square = jnp.mean(widened * widened, axis=-1, keepdims=True)
    normed = (widened * lax.rsqrt(mean_square + 1e-06) * norm_gain.astype(jnp.float32)).astype(
        jnp.bfloat16
    )
    return normed[None]


def solution(mesh):
    return jax.shard_map(
        body,
        mesh=mesh,
        in_specs=(
            P(("groups", "enc"), "ctx", None),
            P(("groups", "enc"), "ctx"),
            P(("groups", "enc"), "ctx"),
            P(None, ("ctx", "tp")),
            P(None, ("ctx", "tp")),
            P(("ctx", "tp")),
            P(("ctx", "tp")),
            P(),
        ),
        out_specs=P(("groups", "enc"), ("ctx", "tp"), None),
        check_vma=False,
    )
```

profile of v0, /device:TPU:0, one launch (start us, length us, event | category | flops | bytes accessed | tf_op | source)
XLA Modules:
  0.0 195.7 jit_solution(15758488479154289342)
XLA Ops:
  6.5 0.0 copy-start
  6.5 0.8 and_select_fusion.3
  7.3 0.7 and_select_fusion.2
  8.0 1.2 reduce-window.6
  9.2 0.1 slice.8
  9.3 0.1 copy.18
  9.4 0.1 copy.19
  9.5 0.1 add_bitcast_fusion
  9.6 0.7 multiply_add_fusion
  10.3 1.5 select_reduce_fusion.2
  11.8 0.6 broadcast_add_fusion
  12.4 6.3 %all-to-all-start = ((s32[4,1,128]{2,1,0:T(1,128)}), s32[4,1,128]{2,1,0:T(1,128)S(1)}, u32[]{:S(2)}, u32[]{:S(2)}) async-start(s32[4,1,128]{2,1,0:T(1,128)} %bitcast.7), calls=%async_computation | async-start | bytes 4096 | tf_op jit(solution)/shard_map/all_to_all | solution.py:42
  18.7 0.0 all-gather.3.cloned.1.call-start
  18.7 0.0 copy-done
  18.7 0.5 convolution_convert_fusion
  19.2 4.9 %all-to-all-done = s32[4,1,128]{2,1,0:T(1,128)S(1)} async-done(((s32[4,1,128]{2,1,0:T(1,128)}), s32[4,1,128]{2,1,0:T(1,128)S(1)}, u32[]{:S(2)}, u32[]{:S(2)}) %all-to-all-start) | async-done | bytes 2080 | tf_op jit(solution)/shard_map/all_to_all | solution.py:42
  24.2 0.0 copy-start.2
  24.2 0.0 copy-start.3
  24.2 32.7 %all_to_all.33 = bf16[4,128,1280]{2,1,0:T(8,128)(2,1)S(1)} all-to-all(bf16[4,128,1280]{2,1,0:T(8,128)(2,1)S(1)} %bitcast.39), channel_id=1, replica_groups=mesh['groups'=2,'ctx'=4,'enc'=2,'tp'=2] {'ctx'}, dimensions={0} | all-to-all | bytes 2621440 | tf_op jit(solution)/shard_map/all_to_all | solution.py:41
  56.9 1.3 convolution_convert_fusion.1
  58.3 0.0 all-gather.3.cloned.1.call-update
  58.3 3.2 %all-to-all-start.1 = ((s32[4,1,128]{2,1,0:T(1,128)}), s32[4,1,128]{2,1,0:T(1,128)S(1)}, u32[]{:S(2)}, u32[]{:S(2)}) async-start(s32[4,1,128]{2,1,0:T(1,128)} %bitcast.10), calls=%async_computation.1 | async-start | bytes 4096 | tf_op jit(solution)/shard_map/all_to_all | solution.py:43
  61.5 0.0 copy-done.2
  61.5 0.0 copy-done.3
  61.6 5.5 %all-to-all-done.1 = s32[4,1,128]{2,1,0:T(1,128)S(1)} async-done(((s32[4,1,128]{2,1,0:T(1,128)}), s32[4,1,128]{2,1,0:T(1,128)S(1)}, u32[]{:S(2)}, u32[]{:S(2)}) %all-to-all-start.1) | async-done | bytes 2080 | tf_op jit(solution)/shard_map/all_to_all | solution.py:43
  67.0 0.1 select_reduce_fusion
  67.2 8.4 %all-gather = s32[4,1,256]{2,1,0:T(1,128)S(1)} all-gather(s32[1,1,256]{2,1,0:T(1,128)S(1)} %bitcast.50), channel_id=1, replica_groups=mesh['groups'=2,'ctx'=4,'enc'=2,'tp'=2] {'ctx'}, dimensions={0}, use_global_device_ids=true | all-gather | bytes 5120 | tf_op jit(solution)/shard_map/all_gather | solution.py:58
  75.5 0.0 copy-start.4
  75.6 36.9 %all-gather.3.cloned.1.call-done = bf16[1024,1280]{1,0:T(8,128)(2,1)} async-done(((bf16[256,1280]{1,0:T(8,128)(2,1)}), bf16[1024,1280]{1,0:T(8,128)(2,1)}) %all-gather.3.cloned.1.call-update) | async-done | bytes 2621456 | tf_op jit(solution)/shard_map/all_gather | solution.py:57
  112.4 0.0 copy-start.5
  112.4 2.4 %broadcast_select_fusion.1 = (bf16[1024,1280]{1,0:T(8,128)(2,1)S(1)}, bf16[1024,1280]{1,0:T(8,128)(2,1)S(1)}) fusion(bf16[1024,1280]{1,0:T(8,128)(2,1)} %all-gather.3.cloned.1.call-done, pred[1024]{0:T(1024)(128)(4,1)S(1)} %reshape.162), kind=kLoop, calls=%fused_computation.14 | loop fusion | flops 2621440 | bytes 7865344 | tf_op jit(solution)/shard_map/jit(_where)/select_n | solution.py:11
  114.8 0.0 copy-done.4
  114.8 0.1 copy-done.5
  114.9 6.9 %add_convert_fusion = bf16[1024,1024]{1,0:T(8,128)(2,1)} fusion(f32[1024]{0:T(1024)S(1)} %convert_element_type.64, f32[1024]{0:T(1024)S(1)} %convert_element_type.63, pred[1024]{0:T(1024)(128)(4,1)S(1)} %reshape.162, bf16[1280,1024]{1,0:T(8,128)(2,1)S(1)} %copy-done.4, bf16[1280,1024]{1,0:T(8,128)(2,1)S(1)} %copy-done.5, ...), kind=kOutput, calls=%fused_computation.11 | convolution fusion | flops 5392826368 | bytes 12592128 | tf_op jit(solution)/shard_map/dot_general | solution.py:13
  121.8 0.0 copy-start.1
  121.8 3.7 %all-to-all-start.3 = ((bf16[8,128,1024]{2,1,0:T(8,128)(2,1)}), bf16[8,128,1024]{2,1,0:T(8,128)(2,1)S(1)}, u32[]{:S(2)}, u32[]{:S(2)}) async-start(bf16[8,128,1024]{2,1,0:T(8,128)(2,1)} %bitcast.41), calls=%async_computation.3 | async-start | bytes 4194304 | tf_op jit(solution)/shard_map/all_to_all | solution.py:63
  125.6 0.0 copy-done.1
  125.6 49.0 %all-to-all-done.3 = bf16[8,128,1024]{2,1,0:T(8,128)(2,1)S(1)} async-done(((bf16[8,128,1024]{2,1,0:T(8,128)(2,1)}), bf16[8,128,1024]{2,1,0:T(8,128)(2,1)S(1)}, u32[]{:S(2)}, u32[]{:S(2)}) %all-to-all-start.3) | async-done | bytes 2097184 | tf_op jit(solution)/shard_map/all_to_all | solution.py:63
  174.6 0.5 fusion.7
  175.1 0.5 convert_bitcast_fusion
  175.5 4.4 %copy.20 = f32[128,8,1024]{2,1,0:T(8,128)} copy(f32[128,8,1024]{2,0,1:T(8,128)S(1)} %convert_bitcast_fusion) | data formatting | bytes 8388608 | tf_op jit(solution)/shard_map/convert_element_type | solution.py:66
  179.9 5.0 %reshape.158 = f32[1,128,8192]{2,1,0:T(8,128)} reshape(f32[128,8,1024]{2,1,0:T(8,128)} %copy.20) | data formatting | bytes 8388608 | tf_op jit(solution)/shard_map/convert_element_type | solution.py:66
  184.9 4.0 %multiply_convert_fusion = bf16[1,128,8192]{2,1,0:T(8,128)(2,1)} fusion(f32[1,128,8192]{2,1,0:T(8,128)} %reshape.158, f32[8192]{0:T(1024)S(1)} %convert_element_type.70, f32[128]{0:T(128)S(1)} %add_rsqrt_fusion), kind=kLoop, calls=%fused_computation.10 | loop fusion | flops 3145728 | bytes 6324736 | tf_op jit(solution)/shard_map/convert_element_type | solution.py:68
  (10 shorter events, 0.1 us)
Async XLA Ops:
  6.5 12.2 %copy-start = (bf16[1,256,1280]{2,1,0:T(8,128)(2,1)S(1)}, bf16[1,256,1280]{2,1,0:T(8,128)(2,1)}, u32[]{:S(2)}) copy-start(bf16[1,256,1280]{2,1,0:T(8,128)(2,1)} %param.8) | copy-start | bytes 1966084
  12.4 11.8 %all-to-all-start = ((s32[4,1,128]{2,1,0:T(1,128)}), s32[4,1,128]{2,1,0:T(1,128)S(1)}, u32[]{:S(2)}, u32[]{:S(2)}) async-start(s32[4,1,128]{2,1,0:T(1,128)} %bitcast.7), calls=%async_computation | async-start | bytes 4096 | tf_op jit(solution)/shard_map/all_to_all | solution.py:42
  18.7 93.7 %all-gather.3.cloned.1.call-start = ((), (), s32[]{:S(2)}) async-start(), calls=%async_computation.4 | async-start | bytes 3276800 | tf_op jit(solution)/shard_map/all_gather | solution.py:57
  24.2 37.3 %copy-start.2 = (bf16[1024]{0:T(1024)(128)(2,1)S(1)}, bf16[1024]{0:T(1024)(128)(2,1)}, u32[]{:S(2)}) copy-start(bf16[1024]{0:T(1024)(128)(2,1)} %param.13) | copy-start | bytes 6148
  24.2 37.3 %copy-start.3 = (bf16[1024]{0:T(1024)(128)(2,1)S(1)}, bf16[1024]{0:T(1024)(128)(2,1)}, u32[]{:S(2)}) copy-start(bf16[1024]{0:T(1024)(128)(2,1)} %param.14) | copy-start | bytes 6148
  58.3 8.7 %all-to-all-start.1 = ((s32[4,1,128]{2,1,0:T(1,128)}), s32[4,1,128]{2,1,0:T(1,128)S(1)}, u32[]{:S(2)}, u32[]{:S(2)}) async-start(s32[4,1,128]{2,1,0:T(1,128)} %bitcast.10), calls=%async_computation.1 | async-start | bytes 4096 | tf_op jit(solution)/shard_map/all_to_all | solution.py:43
  75.5 39.2 %copy-start.4 = (bf16[1280,1024]{1,0:T(8,128)(2,1)S(1)}, bf16[1280,1024]{1,0:T(8,128)(2,1)}, u32[]{:S(2)}) copy-start(bf16[1280,1024]{1,0:T(8,128)(2,1)} %param.12) | copy-start | bytes 7864324
  112.4 2.5 %copy-start.5 = (bf16[1280,1024]{1,0:T(8,128)(2,1)S(1)}, bf16[1280,1024]{1,0:T(8,128)(2,1)}, u32[]{:S(2)}) copy-start(bf16[1280,1024]{1,0:T(8,128)(2,1)} %param.11) | copy-start | bytes 7864324
  121.8 3.7 %copy-start.1 = (bf16[8192]{0:T(1024)(128)(2,1)S(1)}, bf16[8192]{0:T(1024)(128)(2,1)}, u32[]{:S(2)}) copy-start(bf16[8192]{0:T(1024)(128)(2,1)} %param.15) | copy-start | bytes 49156
  121.8 52.7 %all-to-all-start.3 = ((bf16[8,128,1024]{2,1,0:T(8,128)(2,1)}), bf16[8,128,1024]{2,1,0:T(8,128)(2,1)S(1)}, u32[]{:S(2)}, u32[]{:S(2)}) async-start(bf16[8,128,1024]{2,1,0:T(8,128)(2,1)} %bitcast.41), calls=%async_computation.3 | async-start | bytes 4194304 | tf_op jit(solution)/shard_map/all_to_all | solution.py:63
Sparse Core Ops, SparseCore 0:
  58.4 53.9 all-gather.2
where the time goes:
time: 196 us
  waiting for transfers between devices  96.2 us (49%)
  blocking collectives  41.1 us (21%)
  between operations  13.5 us (7%)
  starting transfers between devices  13.2 us (7%)
  other arithmetic  13.1 us (7%)
  local copies, waits for them, and re-layouts  9.79 us (5%)
  matrix products  8.76 us (4%)
    all_to_all x1, waiting for transfers between devices, body(): lax.all_to_all(columns.astype(jnp.bfloat16), ('ctx', 'tp'), split_axis=0,...  49 us
    all_gather x1, waiting for transfers between devices, body(): lax.all_gather(shard_rows, 'ctx', axis=0, tiled=True)  36.9 us
    all_to_all x1, blocking collectives, body(): lax.all_to_all(parcel, 'ctx', split_axis=0, concat_axis=0, tiled=True)  32.7 us
    convert_element_type x2, local copies, waits for them, and re-layouts, body(): widened = embeds.astype(jnp.float32)  9.33 us
    all_gather x1, blocking collectives, body(): lax.all_gather(shard_kind, 'ctx', axis=0, tiled=True)  8.35 us
    dot_general x1, matrix products, project(): result = jnp.dot(stacked, weights, preferred_element_type=jnp.float32)  6.9 us
    all_to_all x1, starting transfers between devices, body(): lax.all_to_all(where_to, 'ctx', split_axis=0, concat_axis=0, tiled=True)  6.32 us
    all_to_all x1, waiting for transfers between devices, body(): lax.all_to_all(what_kind, 'ctx', split_axis=0, concat_axis=0, tiled=True)  5.47 us
  transfers between devices with their start and end apart: 4, of which 4 were waited for; matrix products, arithmetic and copies ran while one was open for 0% of the time, Pallas kernels for 0%

commit v1 on v0

--- a/solution.py
+++ b/solution.py
@@ -2,6 +2,18 @@
 import jax.numpy as jnp
 from jax import lax
 from jax.sharding import PartitionSpec as P
+
+
+def exchange_directly(x, axis, split, join):
+    ways, here = (lax.axis_size(axis), lax.axis_index(axis))
+    width = x.shape[split] // ways
+    turned = jnp.roll(x, -here * width, axis=split)
+    got = [lax.slice_in_dim(turned, 0, width, axis=split)]
+    for far in range(1, ways):
+        sent = lax.slice_in_dim(turned, far * width, (far + 1) * width, axis=split)
+        got.append(lax.ppermute(sent, axis, [(d, (d + far) % ways) for d in range(ways)]))
+    line = jnp.concatenate(got[::-1], axis=join)
+    return jnp.roll(line, (here + 1) * got[0].shape[join], axis=join)
 
 
 def project(enc_part, kind_part, weights, bias_audio, bias_frame):
@@ -38,7 +50,7 @@
     where_to = (jnp.sum(send_int * (position + 1)[None, :], axis=1) - 1).reshape(n_ctx, capacity)
     what_kind = jnp.sum(send_int * owned_kind[None, :], axis=1).reshape(n_ctx, capacity)
     arrived = (
-        lax.all_to_all(parcel, "ctx", split_axis=0, concat_axis=0, tiled=True),
+        exchange_directly(parcel, "ctx", 0, 0),
         lax.all_to_all(where_to, "ctx", split_axis=0, concat_axis=0, tiled=True),
         lax.all_to_all(what_kind, "ctx", split_axis=0, concat_axis=0, tiled=True),
     )

time: 196 us -> 186 us (0.949)
  blocking collectives: 41.1 us -> 8.73 us
  waiting for transfers between devices: 96.2 us -> 112 us
  starting transfers between devices: 13.2 us -> 18.7 us
    all_to_all x1 -> x0, blocking collectives: 32.7 us -> none  [body(): lax.all_to_all(parcel, 'ctx', split_axis=0, concat_axis=0, tiled=True)]
    ppermute x0 -> x3, waiting for transfers between devices: none -> 15.3 us  [exchange_directly(): lax.ppermute(sent, axis, [(d, (d + far) % ways) for d in range(ways)])]
    ppermute x0 -> x3, starting transfers between devices: none -> 7.01 us  [exchange_directly(): lax.ppermute(sent, axis, [(d, (d + far) % ways) for d in range(ways)])]
    all_to_all x1, starting transfers between devices: 6.32 us -> 3.22 us  [body(): lax.all_to_all(where_to, 'ctx', split_axis=0, concat_axis=0, tiled=True)]
    concatenate x0 -> x2, other arithmetic: none -> 2.04 us  [the longest x1 1.55 us: exchange_directly(): return jnp.roll(line, (here + 1) * got[0].shape[join], axis=join)]
  transfers between devices with their start and end apart: 4 -> 7, of which waited for: 4 -> 6; matrix products, arithmetic and copies ran while one was open for 0% -> 2% of each run, Pallas kernels for 0% -> 0%
where the time goes in v1:
time: 186 us
  waiting for transfers between devices  112 us (60%)
  starting transfers between devices  18.7 us (10%)
  other arithmetic  14.4 us (8%)
  between operations  13.6 us (7%)
  local copies, waits for them, and re-layouts  9.89 us (5%)
  matrix products  8.76 us (5%)
  blocking collectives  8.73 us (5%)
    all_to_all x1, waiting for transfers between devices, body(): lax.all_to_all(columns.astype(jnp.bfloat16), ('ctx', 'tp'), split_axis=0,...  48.8 us
    all_gather x1, waiting for transfers between devices, body(): lax.all_gather(shard_rows, 'ctx', axis=0, tiled=True)  36.8 us
    ppermute x3, waiting for transfers between devices, exchange_directly(): lax.ppermute(sent, axis, [(d, (d + far) % ways) for d in range(ways)])  15.3 us
    convert_element_type x2, local copies, waits for them, and re-layouts, body(): widened = embeds.astype(jnp.float32)  9.33 us
    all_gather x1, blocking collectives, body(): lax.all_gather(shard_kind, 'ctx', axis=0, tiled=True)  8.73 us
    ppermute x3, starting transfers between devices, exchange_directly(): lax.ppermute(sent, axis, [(d, (d + far) % ways) for d in range(ways)])  7.01 us
    dot_general x1, matrix products, project(): result = jnp.dot(stacked, weights, preferred_element_type=jnp.float32)  6.9 us
    all_to_all x1, waiting for transfers between devices, body(): lax.all_to_all(what_kind, 'ctx', split_axis=0, concat_axis=0, tiled=True)  5.52 us
  transfers between devices with their start and end apart: 7, of which 6 were waited for; matrix products, arithmetic and copies ran while one was open for 2% of the time, Pallas kernels for 0%

profile of v1, /device:TPU:0, one launch (start us, length us, event | category | flops | bytes accessed | tf_op | source)
XLA Modules:
  0.0 185.9 jit_solution(11107481050012932330)
XLA Ops:
  6.5 0.0 copy-start
  6.5 0.8 and_select_fusion.3
  7.3 0.7 and_select_fusion.2
  8.0 1.2 reduce-window.6
  9.2 0.1 slice.24
  9.3 0.1 copy.18
  9.4 0.1 copy.19
  9.5 0.1 add_bitcast_fusion
  9.6 0.7 multiply_add_fusion
  10.3 0.0 copy-done
  10.3 0.5 convolution_convert_fusion
  10.9 0.0 copy-start.4
  10.9 0.5 fusion.19
  11.4 0.1 fusion.28
  11.5 3.1 %collective-permute-start.2 = (bf16[1,128,1280]{2,1,0:T(8,128)(2,1)S(1)}, bf16[1,128,1280]{2,1,0:T(8,128)(2,1)S(1)}, u32[]{:S(2)}, u32[]{:S(2)}) collective-permute-start(bf16[1,128,1280]{2,1,0:T(8,128)(2,1)S(1)} %get-tuple-element.11), channel_id=1, source_target_pairs={{0,4},{4,8},{8,12},{12,0},{1,5},{5,9},{9,13},{13,1},{2,6},{6,10},{... | collective-permute-start | bytes 983048 | tf_op jit(solution)/shard_map/ppermute | solution.py:14
  14.5 2.6 %collective-permute-start.1 = (bf16[1,128,1280]{2,1,0:T(8,128)(2,1)S(1)}, bf16[1,128,1280]{2,1,0:T(8,128)(2,1)S(1)}, u32[]{:S(2)}, u32[]{:S(2)}) collective-permute-start(bf16[1,128,1280]{2,1,0:T(8,128)(2,1)S(1)} %get-tuple-element.12), channel_id=1, source_target_pairs={{0,8},{4,12},{8,0},{12,4},{1,9},{5,13},{9,1},{13,5},{2,10},{6,14},... | collective-permute-start | bytes 983048 | tf_op jit(solution)/shard_map/ppermute | solution.py:14
  17.1 1.3 collective-permute-start
  18.5 0.0 copy-done.4
  18.5 0.8 select_reduce_fusion.2
  19.3 0.6 broadcast_add_fusion
  19.9 3.2 %all-to-all-start = ((s32[4,1,128]{2,1,0:T(1,128)}), s32[4,1,128]{2,1,0:T(1,128)S(1)}, u32[]{:S(2)}, u32[]{:S(2)}) async-start(s32[4,1,128]{2,1,0:T(1,128)} %bitcast.7), calls=%async_computation | async-start | bytes 4096 | tf_op jit(solution)/shard_map/all_to_all | solution.py:54
  23.1 0.0 all-gather.3.cloned.1.call-start
  23.2 2.1 %collective-permute-done.2 = bf16[1,128,1280]{2,1,0:T(8,128)(2,1)S(1)} collective-permute-done((bf16[1,128,1280]{2,1,0:T(8,128)(2,1)S(1)}, bf16[1,128,1280]{2,1,0:T(8,128)(2,1)S(1)}, u32[]{:S(2)}, u32[]{:S(2)}) %collective-permute-start.2) | collective-permute-done | bytes 327712 | tf_op jit(solution)/shard_map/ppermute | solution.py:14
  25.2 13.2 %collective-permute-done.1 = bf16[1,128,1280]{2,1,0:T(8,128)(2,1)S(1)} collective-permute-done((bf16[1,128,1280]{2,1,0:T(8,128)(2,1)S(1)}, bf16[1,128,1280]{2,1,0:T(8,128)(2,1)S(1)}, u32[]{:S(2)}, u32[]{:S(2)}) %collective-permute-start.1) | collective-permute-done | bytes 327712 | tf_op jit(solution)/shard_map/ppermute | solution.py:14
  38.5 0.0 collective-permute-done
  38.5 0.0 copy-start.2
  38.5 0.0 copy-start.3
  38.5 1.6 fusion.15
  40.0 5.4 %all-to-all-done = s32[4,1,128]{2,1,0:T(1,128)S(1)} async-done(((s32[4,1,128]{2,1,0:T(1,128)}), s32[4,1,128]{2,1,0:T(1,128)S(1)}, u32[]{:S(2)}, u32[]{:S(2)}) %all-to-all-start) | async-done | bytes 2080 | tf_op jit(solution)/shard_map/all_to_all | solution.py:54
  45.4 1.3 convolution_convert_fusion.1
  46.7 0.0 all-gather.3.cloned.1.call-update
  46.8 4.5 %all-to-all-start.1 = ((s32[4,1,128]{2,1,0:T(1,128)}), s32[4,1,128]{2,1,0:T(1,128)S(1)}, u32[]{:S(2)}, u32[]{:S(2)}) async-start(s32[4,1,128]{2,1,0:T(1,128)} %bitcast.10), calls=%async_computation.1 | async-start | bytes 4096 | tf_op jit(solution)/shard_map/all_to_all | solution.py:55
  51.3 0.0 copy-done.2
  51.3 0.0 copy-done.3
  51.3 5.5 %all-to-all-done.1 = s32[4,1,128]{2,1,0:T(1,128)S(1)} async-done(((s32[4,1,128]{2,1,0:T(1,128)}), s32[4,1,128]{2,1,0:T(1,128)S(1)}, u32[]{:S(2)}, u32[]{:S(2)}) %all-to-all-start.1) | async-done | bytes 2080 | tf_op jit(solution)/shard_map/all_to_all | solution.py:55
  56.8 0.1 select_reduce_fusion
  56.9 8.7 %all-gather = s32[4,1,256]{2,1,0:T(1,128)S(1)} all-gather(s32[1,1,256]{2,1,0:T(1,128)S(1)} %bitcast.49), channel_id=1, replica_groups=mesh['groups'=2,'ctx'=4,'enc'=2,'tp'=2] {'ctx'}, dimensions={0}, use_global_device_ids=true | all-gather | bytes 5120 | tf_op jit(solution)/shard_map/all_gather | solution.py:70
  65.7 0.0 copy-start.5
  65.7 36.8 %all-gather.3.cloned.1.call-done = bf16[1024,1280]{1,0:T(8,128)(2,1)} async-done(((bf16[256,1280]{1,0:T(8,128)(2,1)}), bf16[1024,1280]{1,0:T(8,128)(2,1)}) %all-gather.3.cloned.1.call-update) | async-done | bytes 2621456 | tf_op jit(solution)/shard_map/all_gather | solution.py:69
  102.6 0.0 copy-start.6
  102.6 2.4 %broadcast_select_fusion.1 = (bf16[1024,1280]{1,0:T(8,128)(2,1)S(1)}, bf16[1024,1280]{1,0:T(8,128)(2,1)S(1)}) fusion(bf16[1024,1280]{1,0:T(8,128)(2,1)} %all-gather.3.cloned.1.call-done, pred[1024]{0:T(1024)(128)(4,1)S(1)} %reshape.162), kind=kLoop, calls=%fused_computation.24 | loop fusion | flops 2621440 | bytes 7865344 | tf_op jit(solution)/shard_map/jit(_where)/select_n | solution.py:23
  104.9 0.0 copy-done.5
  104.9 0.1 copy-done.6
  105.1 6.9 %add_convert_fusion = bf16[1024,1024]{1,0:T(8,128)(2,1)} fusion(f32[1024]{0:T(1024)S(1)} %convert_element_type.64, f32[1024]{0:T(1024)S(1)} %convert_element_type.63, pred[1024]{0:T(1024)(128)(4,1)S(1)} %reshape.162, bf16[1280,1024]{1,0:T(8,128)(2,1)S(1)} %copy-done.5, bf16[1280,1024]{1,0:T(8,128)(2,1)S(1)} %copy-done.6, ...), kind=kOutput, calls=%fused_computation.11 | convolution fusion | flops 5392826368 | bytes 12592128 | tf_op jit(solution)/shard_map/dot_general | solution.py:25
  112.0 0.0 copy-start.1
  112.0 3.9 %all-to-all-start.2 = ((bf16[8,128,1024]{2,1,0:T(8,128)(2,1)}), bf16[8,128,1024]{2,1,0:T(8,128)(2,1)S(1)}, u32[]{:S(2)}, u32[]{:S(2)}) async-start(bf16[8,128,1024]{2,1,0:T(8,128)(2,1)} %bitcast.41), calls=%async_computation.2 | async-start | bytes 4194304 | tf_op jit(solution)/shard_map/all_to_all | solution.py:75
  115.9 0.0 copy-done.1
  115.9 48.8 %all-to-all-done.2 = bf16[8,128,1024]{2,1,0:T(8,128)(2,1)S(1)} async-done(((bf16[8,128,1024]{2,1,0:T(8,128)(2,1)}), bf16[8,128,1024]{2,1,0:T(8,128)(2,1)S(1)}, u32[]{:S(2)}, u32[]{:S(2)}) %all-to-all-start.2) | async-done | bytes 2097184 | tf_op jit(solution)/shard_map/all_to_all | solution.py:75
  164.7 0.5 fusion.7
  165.2 0.5 convert_bitcast_fusion
  165.7 4.4 %copy.20 = f32[128,8,1024]{2,1,0:T(8,128)} copy(f32[128,8,1024]{2,0,1:T(8,128)S(1)} %convert_bitcast_fusion) | data formatting | bytes 8388608 | tf_op jit(solution)/shard_map/convert_element_type | solution.py:78
  170.1 5.0 %reshape.158 = f32[1,128,8192]{2,1,0:T(8,128)} reshape(f32[128,8,1024]{2,1,0:T(8,128)} %copy.20) | data formatting | bytes 8388608 | tf_op jit(solution)/shard_map/convert_element_type | solution.py:78
  175.0 4.0 %multiply_convert_fusion = bf16[1,128,8192]{2,1,0:T(8,128)(2,1)} fusion(f32[1,128,8192]{2,1,0:T(8,128)} %reshape.158, f32[8192]{0:T(1024)S(1)} %convert_element_type.70, f32[128]{0:T(128)S(1)} %add_rsqrt_fusion), kind=kLoop, calls=%fused_computation.10 | loop fusion | flops 3145728 | bytes 6324736 | tf_op jit(solution)/shard_map/convert_element_type | solution.py:80
  (10 shorter events, 0.1 us)
Async XLA Ops:
  6.5 3.8 %copy-start = (bf16[1,256,1280]{2,1,0:T(8,128)(2,1)S(1)}, bf16[1,256,1280]{2,1,0:T(8,128)(2,1)}, u32[]{:S(2)}) copy-start(bf16[1,256,1280]{2,1,0:T(8,128)(2,1)} %param.10) | copy-start | bytes 1966084
  10.9 7.6 %copy-start.4 = (s32[1,256]{1,0:T(1,128)S(1)}, s32[1,256]{1,0:T(1,128)}, u32[]{:S(2)}) copy-start(s32[1,256]{1,0:T(1,128)} %param.12) | copy-start | bytes 3076
  11.5 13.8 %collective-permute-start.2 = (bf16[1,128,1280]{2,1,0:T(8,128)(2,1)S(1)}, bf16[1,128,1280]{2,1,0:T(8,128)(2,1)S(1)}, u32[]{:S(2)}, u32[]{:S(2)}) collective-permute-start(bf16[1,128,1280]{2,1,0:T(8,128)(2,1)S(1)} %get-tuple-element.11), channel_id=1, source_target_pairs={{0,4},{4,8},{8,12},{12,0},{1,5},{5,9},{9,13},{13,1},{2,6},{6,10},{... | collective-permute-start | bytes 983048 | tf_op jit(solution)/shard_map/ppermute | solution.py:14
  14.5 23.9 %collective-permute-start.1 = (bf16[1,128,1280]{2,1,0:T(8,128)(2,1)S(1)}, bf16[1,128,1280]{2,1,0:T(8,128)(2,1)S(1)}, u32[]{:S(2)}, u32[]{:S(2)}) collective-permute-start(bf16[1,128,1280]{2,1,0:T(8,128)(2,1)S(1)} %get-tuple-element.12), channel_id=1, source_target_pairs={{0,8},{4,12},{8,0},{12,4},{1,9},{5,13},{9,1},{13,5},{2,10},{6,14},... | collective-permute-start | bytes 983048 | tf_op jit(solution)/shard_map/ppermute | solution.py:14
  17.1 21.4 %collective-permute-start = (bf16[1,128,1280]{2,1,0:T(8,128)(2,1)S(1)}, bf16[1,128,1280]{2,1,0:T(8,128)(2,1)S(1)}, u32[]{:S(2)}, u32[]{:S(2)}) collective-permute-start(bf16[1,128,1280]{2,1,0:T(8,128)(2,1)S(1)} %get-tuple-element.13), channel_id=1, source_target_pairs={{0,12},{4,0},{8,4},{12,8},{1,13},{5,1},{9,5},{13,9},{2,14},{6,2},{... | collective-permute-start | bytes 983048 | tf_op jit(solution)/shard_map/ppermute | solution.py:14
  19.9 25.5 %all-to-all-start = ((s32[4,1,128]{2,1,0:T(1,128)}), s32[4,1,128]{2,1,0:T(1,128)S(1)}, u32[]{:S(2)}, u32[]{:S(2)}) async-start(s32[4,1,128]{2,1,0:T(1,128)} %bitcast.7), calls=%async_computation | async-start | bytes 4096 | tf_op jit(solution)/shard_map/all_to_all | solution.py:54
  23.1 79.4 %all-gather.3.cloned.1.call-start = ((), (), s32[]{:S(2)}) async-start(), calls=%async_computation.3 | async-start | bytes 3276800 | tf_op jit(solution)/shard_map/all_gather | solution.py:69
  38.5 12.8 %copy-start.2 = (bf16[1024]{0:T(1024)(128)(2,1)S(1)}, bf16[1024]{0:T(1024)(128)(2,1)}, u32[]{:S(2)}) copy-start(bf16[1024]{0:T(1024)(128)(2,1)} %param.15) | copy-start | bytes 6148
  38.5 12.8 %copy-start.3 = (bf16[1024]{0:T(1024)(128)(2,1)S(1)}, bf16[1024]{0:T(1024)(128)(2,1)}, u32[]{:S(2)}) copy-start(bf16[1024]{0:T(1024)(128)(2,1)} %param.16) | copy-start | bytes 6148
  46.8 10.0 %all-to-all-start.1 = ((s32[4,1,128]{2,1,0:T(1,128)}), s32[4,1,128]{2,1,0:T(1,128)S(1)}, u32[]{:S(2)}, u32[]{:S(2)}) async-start(s32[4,1,128]{2,1,0:T(1,128)} %bitcast.10), calls=%async_computation.1 | async-start | bytes 4096 | tf_op jit(solution)/shard_map/all_to_all | solution.py:55
  65.7 39.2 %copy-start.5 = (bf16[1280,1024]{1,0:T(8,128)(2,1)S(1)}, bf16[1280,1024]{1,0:T(8,128)(2,1)}, u32[]{:S(2)}) copy-start(bf16[1280,1024]{1,0:T(8,128)(2,1)} %param.14) | copy-start | bytes 7864324
  102.6 2.5 %copy-start.6 = (bf16[1280,1024]{1,0:T(8,128)(2,1)S(1)}, bf16[1280,1024]{1,0:T(8,128)(2,1)}, u32[]{:S(2)}) copy-start(bf16[1280,1024]{1,0:T(8,128)(2,1)} %param.13) | copy-start | bytes 7864324
  112.0 3.9 %copy-start.1 = (bf16[8192]{0:T(1024)(128)(2,1)S(1)}, bf16[8192]{0:T(1024)(128)(2,1)}, u32[]{:S(2)}) copy-start(bf16[8192]{0:T(1024)(128)(2,1)} %param.17) | copy-start | bytes 49156
  112.0 52.7 %all-to-all-start.2 = ((bf16[8,128,1024]{2,1,0:T(8,128)(2,1)}), bf16[8,128,1024]{2,1,0:T(8,128)(2,1)S(1)}, u32[]{:S(2)}, u32[]{:S(2)}) async-start(bf16[8,128,1024]{2,1,0:T(8,128)(2,1)} %bitcast.41), calls=%async_computation.2 | async-start | bytes 4194304 | tf_op jit(solution)/shard_map/all_to_all | solution.py:75
Sparse Core Ops, SparseCore 0:
  46.9 55.6 all-gather.2
